TPU v7x, 256 devices: a whole 4x4x8 slice. The times are simulated.
256 devices in a mesh: shuf: 4 (over y_lo, core), key: 64 (over x, z, y_hi).
Axes of the slice: x: 4, y: 4 (y_hi: 2, y_lo: 2; y = y_hi * 2 + y_lo), z: 8, core: 2. Of those that a mesh axis runs over, the one named last changes fastest.
Arguments:
- embeddings: bfloat16 [32768, 1024], P(('shuf', 'key')), may hold values from -200 to 200
- labels: int32 [32768], P(('shuf', 'key')), may hold values from 0 to 2047
- order: int32 [256, 128], P(('shuf', 'key')), may hold values from 0 to 127, each once within a row
- head_weight: bfloat16 [1024, 512], replicated, may hold values from -0.1875 to 0.1875
Outputs:
- grad_embeddings: bfloat16 [32768, 1024], P(('shuf', 'key'))
- grad_head: float32 [1024, 512], P('key')
All inputs are finite; a program needn't handle non-finite values.
Results may differ from a plain program's by a relative error of at most 0.0075.
Values may be sent and summed in bfloat16 or wider, within the bound.
No kernel may reach another device: no remote copies, remote signals or barrier semaphores. Data moves between devices by JAX's collectives and lax.ppermute only.
A program may use at most 64 MiB of HBM per device.

v0:
```python
import jax
import jax.numpy as jnp
from jax import lax
from jax.sharding import PartitionSpec as P

exponent_divisor = 0.1
loss_scale = 64.0
epsilon = 1e-06


def tile_terms(query_embeddings, anchor_labels, anchor_index, piece_keys, piece_labels):
    piece_rows = piece_keys.shape[0]
    cosine_score_table = (
        lax.dot_general(
            query_embeddings,
            piece_keys,
            (((1,), (1,)), ((), ())),
            preferred_element_type=jnp.float32,
        )
        / exponent_divisor
    )
    column = jnp.arange(piece_rows, dtype=jnp.int32)
    itself = anchor_index[:, None] == column[None, :]
    exponent = jnp.where(itself, 0.0, jnp.exp(cosine_score_table))
    positive = jnp.logical_and(
        anchor_labels[:, None] == piece_labels[None, :], jnp.logical_not(itself)
    ).astype(jnp.float32)
    return (exponent, positive)


def body(embeddings, labels, order, head_weight):
    row_count = embeddings.shape[0]
    routing = order[0]
    sent_rows = jnp.take(embeddings, routing, axis=0)
    sent_labels = jnp.take(labels, routing, axis=0)
    group_rows, group_labels = (
        lax.all_to_all(sent_rows, "shuf", split_axis=0, concat_axis=0, tiled=True),
        lax.all_to_all(sent_labels, "shuf", split_axis=0, concat_axis=0, tiled=True),
    )
    projected = jnp.dot(group_rows, head_weight, preferred_element_type=jnp.float32)
    row_norm = jnp.sqrt(jnp.sum(projected * projected, axis=1, keepdims=True) + epsilon)
    direction = projected / row_norm
    normed = direction.astype(jnp.bfloat16)
    anchor_index = lax.axis_index("key") * row_count + jnp.arange(row_count, dtype=jnp.int32)
    pieces = (
        lax.all_gather(normed, "key", axis=0, tiled=True),
        lax.all_gather(group_labels, "key", axis=0, tiled=True),
    )
    exponent, positive = tile_terms(normed, group_labels, anchor_index, pieces[0], pieces[1])
    totals = jnp.sum(exponent, axis=1)
    counts = jnp.sum(positive, axis=1)
    floor_count = jnp.maximum(counts, 1.0)
    soft_weight = loss_scale * counts / (floor_count * totals)
    pos_weight = loss_scale / floor_count
    all_soft, all_pos = (
        lax.all_gather(soft_weight, "key", axis=0, tiled=True),
        lax.all_gather(pos_weight, "key", axis=0, tiled=True),
    )
    pieces = (
        lax.all_gather(normed, "key", axis=0, tiled=True),
        lax.all_gather(group_labels, "key", axis=0, tiled=True),
    )
    exponent, positive = tile_terms(normed, group_labels, anchor_index, pieces[0], pieces[1])
    coefficient = (
        (soft_weight[:, None] + all_soft[None, :]) * exponent
        - (pos_weight[:, None] + all_pos[None, :]) * positive
    ).astype(jnp.bfloat16)
    positive_partner = jnp.dot(coefficient, pieces[0], preferred_element_type=jnp.float32)
    positive_pull_derivative = positive_partner / exponent_divisor
    along = jnp.sum(direction * positive_pull_derivative, axis=1, keepdims=True)
    slopes = ((positive_pull_derivative - direction * along) / row_norm).astype(jnp.bfloat16)
    grad_rows = lax.dot_general(
        slopes, head_weight, (((1,), (1,)), ((), ())), preferred_element_type=jnp.float32
    ).astype(jnp.bfloat16)
    returned = lax.all_to_all(grad_rows, "shuf", split_axis=0, concat_axis=0, tiled=True)
    grad_embeddings = jnp.zeros_like(embeddings).at[routing].set(returned)
    summed_all = lax.psum(
        lax.dot_general(
            group_rows, slopes, (((0,), (0,)), ((), ())), preferred_element_type=jnp.float32
        ).astype(jnp.bfloat16),
        "shuf",
    ).astype(jnp.float32)
    grad_head = lax.psum_scatter(summed_all, "key", scatter_dimension=0, tiled=True)
    return (grad_embeddings, grad_head / loss_scale)


def solution(mesh):
    return jax.shard_map(
        body,
        mesh=mesh,
        in_specs=(P(("shuf", "key"), None), P(("shuf", "key")), P(("shuf", "key"), None), P()),
        out_specs=(P(("shuf", "key"), None), P("key", None)),
        check_vma=False,
    )
```

profile of v0, /device:TPU:8, one launch (start us, length us, event | category | flops | bytes accessed | tf_op | source)
XLA Modules:
  0.0 990.7 jit_solution(10155050195612298073)
XLA Ops:
  7.2 0.7 fusion.16
  8.0 0.7 squeeze.9
  8.7 2.0 gather_fusion.1
  10.9 8.9 all_to_all.27
  20.2 0.8 fusion.18
  21.5 0.6 reduce.10
  22.2 1.2 gather_fusion
  23.5 0.6 and_select_fusion
  24.1 4.9 all-to-all-start
  28.9 1.7 all-to-all-done
  30.7 0.6 reduce.11
  31.4 181.5 %all-gather = s32[64,1,128]{2,1,0:T(1,128)S(1)} all-gather(s32[1,1,128]{2,1,0:T(1,128)S(1)} %reshape.148), channel_id=1, replica_groups=mesh['shuf'=4,'key'=64] {'key'}, dimensions={0}, use_global_device_ids=true | all-gather | bytes 33280 | tf_op jit(solution)/shard_map/all_gather | solution.py:47
  212.8 1.4 convert_reduce_fusion
  214.2 6.6 fusion.19
  220.9 173.1 %all-gather.2 = f32[64,1,128]{2,1,0:T(1,128)S(1)} all-gather(f32[1,1,128]{2,1,0:T(1,128)S(1)} %bitcast.36), channel_id=1, replica_groups=mesh['shuf'=4,'key'=64] {'key'}, dimensions={0}, use_global_device_ids=true | all-gather | bytes 33280 | tf_op jit(solution)/shard_map/all_gather | solution.py:57
  394.0 176.6 %all-gather.1 = f32[64,1,128]{2,1,0:T(1,128)S(1)} all-gather(f32[1,1,128]{2,1,0:T(1,128)S(1)} %bitcast.35), channel_id=1, replica_groups=mesh['shuf'=4,'key'=64] {'key'}, dimensions={0}, use_global_device_ids=true | all-gather | bytes 33280 | tf_op jit(solution)/shard_map/all_gather | solution.py:56
  570.6 2.3 multiply_reduce_fusion
  572.9 1.5 convolution_convert_fusion
  574.5 39.0 %all-reduce.2.cloned.1.call-done = bf16[1024,512]{1,0:T(8,128)(2,1)} async-done(((bf16[1024,512]{1,0:T(8,128)(2,1)}), bf16[1024,512]{1,0:T(8,128)(2,1)}) %all-reduce.2.cloned.1.call-update) | async-done | bytes 1048592 | tf_op jit(solution)/shard_map/psum | solution.py:77
  613.5 2.9 convert_element_type.28
  616.9 7.9 all_to_all.28
  624.8 1.8 scatter_custom_fusion
  626.6 356.3 %reduce-scatter.2.cloned.1.call-done = f32[16,512]{1,0:T(8,128)} async-done(((f32[1024,512]{1,0:T(8,128)}), f32[16,512]{1,0:T(8,128)}) %reduce-scatter.2.cloned.1.call-update) | async-done | bytes 32784 | tf_op jit(solution)/shard_map/reduce_scatter | solution.py:83
  982.8 1.4 broadcast_multiply_fusion
  (28 shorter events, 2.0 us)
Async XLA Ops:
  7.2 12.7 %copy-start = (bf16[1024,512]{1,0:T(8,128)(2,1)S(1)}, bf16[1024,512]{1,0:T(8,128)(2,1)}, u32[]{:S(2)}) copy-start(bf16[1024,512]{1,0:T(8,128)(2,1)} %param.7) | copy-start | bytes 3145732
  7.2 14.3 %copy-start.2 = (s32[1,128]{1,0:T(1,128)S(1)}, s32[1,128]{1,0:T(1,128)}, u32[]{:S(2)}) copy-start(s32[1,128]{1,0:T(1,128)} %param.6) | copy-start | bytes 1540
  7.2 15.0 %copy-start.1 = (s32[128]{0:T(128)S(1)}, s32[128]{0:T(128)}, u32[]{:S(2)}) copy-start(s32[128]{0:T(128)} %param.5) | copy-start | bytes 1540
  7.2 207.0 %all-gather.5.cloned.1.call-start = ((), (), s32[]{:S(2)}) async-start(), calls=%async_computation.4 | async-start | bytes 8519680 | tf_op jit(solution)/shard_map/all_gather | solution.py:46
  24.1 6.5 all-to-all-start
  28.9 584.6 %all-reduce.2.cloned.1.call-start = ((), (), s32[]{:S(2)}) async-start(), calls=%async_computation.5 | async-start | bytes 2097152 | tf_op jit(solution)/shard_map/psum | solution.py:77
  214.2 356.4 %copy-start.3 = (bf16[8192,512]{1,0:T(8,128)(2,1)S(1)}, bf16[8192,512]{1,0:T(8,128)(2,1)}, u32[]{:S(2)}) copy-start(bf16[8192,512]{1,0:T(8,128)(2,1)} %all-gather.5.cloned.1.call-done) | copy-start | bytes 25165828
  574.5 408.4 %reduce-scatter.2.cloned.1.call-start = ((), (), s32[]{:S(2)}) async-start(), calls=%async_computation.6 | async-start | bytes 2129920 | tf_op jit(solution)/shard_map/reduce_scatter | solution.py:83
Sparse Core Ops, SparseCore 0:
  21.1 148.5 all-gather.4
  574.6 38.8 all-reduce.1
  616.5 366.2 reduce-scatter.1
where the time goes:
time: 991 us
  blocking collectives  548 us (55%)
  waiting for transfers between devices  397 us (40%)
  between operations  13.8 us (1%)
  matrix products  11.3 us (1%)
    reduce_scatter x1, waiting for transfers between devices, body(): lax.psum_scatter(summed_all, 'key', scatter_dimension=0, tiled=True)  356 us
    all_gather x1, blocking collectives, body(): lax.all_gather(group_labels, 'key', axis=0, tiled=True)  181 us
    all_gather x1, blocking collectives, body(): lax.all_gather(soft_weight, 'key', axis=0, tiled=True)  177 us
    all_gather x1, blocking collectives, body(): lax.all_gather(pos_weight, 'key', axis=0, tiled=True)  173 us
    psum x1, waiting for transfers between devices, body(): lax.psum(lax.dot_general(group_rows, slopes, (((0,), (0,)), ((), ())), pr...  39 us
  transfers between devices with their start and end apart: 4, of which 3 were waited for; matrix products, arithmetic and copies ran while one was open for 1% of the time, Pallas kernels for 0%

commit v1 on v0

--- a/solution.py
+++ b/solution.py
@@ -54,7 +54,9 @@
     pos_weight = loss_scale / floor_count
     all_soft, all_pos = (
         lax.all_gather(soft_weight, "key", axis=0, tiled=True),
-        lax.all_gather(pos_weight, "key", axis=0, tiled=True),
+        jnp.concatenate(
+            lax.all_to_all(jnp.stack([pos_weight] * lax.axis_size("key")), "key", 0, 0), axis=0
+        ),
     )
     pieces = (
         lax.all_gather(normed, "key", axis=0, tiled=True),

time: 991 us -> 834 us (0.84)
  blocking collectives: 548 us -> 379 us
    all_gather x1 -> x0, blocking collectives: 173 us -> none  [body(): lax.all_gather(pos_weight, 'key', axis=0, tiled=True)]
  transfers between devices with their start and end apart: 4 -> 5, of which waited for: 3 -> 3; matrix products, arithmetic and copies ran while one was open for 1% -> 1% of each run, Pallas kernels for 0% -> 0%
where the time goes in v1:
time: 834 us
  waiting for transfers between devices  397 us (48%)
  blocking collectives  379 us (45%)
  matrix products  17.6 us (2%)
  between operations  13.8 us (2%)
  starting transfers between devices  9.57 us (1%)
  other arithmetic  8.99 us (1%)
    reduce_scatter x1, waiting for transfers between devices, body(): lax.psum_scatter(summed_all, 'key', scatter_dimension=0, tiled=True)  356 us
    all_gather x1, blocking collectives, body(): lax.all_gather(group_labels, 'key', axis=0, tiled=True)  181 us
    all_gather x1, blocking collectives, body(): lax.all_gather(soft_weight, 'key', axis=0, tiled=True)  181 us
    psum x1, waiting for transfers between devices, body(): lax.psum(lax.dot_general(group_rows, slopes, (((0,), (0,)), ((), ())), pr...  39.2 us
  transfers between devices with their start and end apart: 5, of which 3 were waited for; matrix products, arithmetic and copies ran while one was open for 1% of the time, Pallas kernels for 0%

profile of v1, /device:TPU:8, one launch (start us, length us, event | category | flops | bytes accessed | tf_op | source)
XLA Modules:
  0.0 833.5 jit_solution(3737672986153818868)
XLA Ops:
  7.2 0.7 fusion.16
  8.0 0.7 squeeze.9
  8.7 2.0 gather_fusion.1
  10.9 8.9 %all_to_all.33 = bf16[4,32,1024]{2,1,0:T(8,128)(2,1)S(1)} all-to-all(bf16[4,32,1024]{2,1,0:T(8,128)(2,1)S(1)} %broadcast_select_fusion), channel_id=1, replica_groups=mesh['shuf'=4,'key'=64] {'shuf'}, dimensions={0} | all-to-all | bytes 524288 | tf_op jit(solution)/shard_map/all_to_all | solution.py:37
  20.2 0.8 fusion.18
  22.2 1.2 gather_fusion
  23.5 0.6 and_select_fusion
  24.1 4.9 all-to-all-start
  28.9 1.7 all-to-all-done
  30.7 0.6 reduce.11
  31.4 181.5 %all-gather = s32[64,1,128]{2,1,0:T(1,128)S(1)} all-gather(s32[1,1,128]{2,1,0:T(1,128)S(1)} %reshape.155), channel_id=1, replica_groups=mesh['shuf'=4,'key'=64] {'key'}, dimensions={0}, use_global_device_ids=true | all-gather | bytes 33280 | tf_op jit(solution)/shard_map/all_gather | solution.py:47
  212.8 1.4 convert_reduce_fusion
  214.2 8.4 %fusion.19 = (f32[128]{0:T(128)S(1)}, f32[128,8192]{1,0:T(8,128)}) fusion(bf16[128,512]{1,0:T(8,128)(2,1)} %fusion.18, bf16[8192,512]{1,0:T(8,128)(2,1)} %all-gather.4.cloned.1.call-done, s32[128]{0:T(128)S(1)} %iota_add_fusion), kind=kOutput, calls=%fused_computation.44 | convolution fusion | flops 1077936000 | bytes 12715008 | tf_op jit(solution)/shard_map/dot_general | solution.py:14
  222.7 0.6 stack.2
  223.3 4.6 all-to-all-start.2
  227.9 180.7 %all-gather.1 = f32[64,1,128]{2,1,0:T(1,128)S(1)} all-gather(f32[1,1,128]{2,1,0:T(1,128)S(1)} %bitcast.34), channel_id=1, replica_groups=mesh['shuf'=4,'key'=64] {'key'}, dimensions={0}, use_global_device_ids=true | all-gather | bytes 33280 | tf_op jit(solution)/shard_map/all_gather | solution.py:56
  408.7 6.8 multiply_reduce_fusion
  415.5 1.5 convolution_convert_fusion
  417.1 39.2 %all-reduce.2.cloned.1.call-done = bf16[1024,512]{1,0:T(8,128)(2,1)} async-done(((bf16[1024,512]{1,0:T(8,128)(2,1)}), bf16[1024,512]{1,0:T(8,128)(2,1)}) %all-reduce.2.cloned.1.call-update) | async-done | bytes 1048592 | tf_op jit(solution)/shard_map/psum | solution.py:79
  456.2 2.9 convert_element_type.28
  459.6 7.9 all_to_all.34
  467.5 1.8 scatter_custom_fusion
  469.3 356.3 %reduce-scatter.2.cloned.1.call-done = f32[16,512]{1,0:T(8,128)} async-done(((f32[1024,512]{1,0:T(8,128)}), f32[16,512]{1,0:T(8,128)}) %reduce-scatter.2.cloned.1.call-update) | async-done | bytes 32784 | tf_op jit(solution)/shard_map/reduce_scatter | solution.py:85
  825.6 1.4 broadcast_multiply_fusion
  (28 shorter events, 2.6 us)
Async XLA Ops:
  7.2 12.7 %copy-start = (bf16[1024,512]{1,0:T(8,128)(2,1)S(1)}, bf16[1024,512]{1,0:T(8,128)(2,1)}, u32[]{:S(2)}) copy-start(bf16[1024,512]{1,0:T(8,128)(2,1)} %param.7) | copy-start | bytes 3145732
  7.2 14.3 %copy-start.2 = (s32[1,128]{1,0:T(1,128)S(1)}, s32[1,128]{1,0:T(1,128)}, u32[]{:S(2)}) copy-start(s32[1,128]{1,0:T(1,128)} %param.6) | copy-start | bytes 1540
  7.2 15.0 %copy-start.1 = (s32[128]{0:T(128)S(1)}, s32[128]{0:T(128)}, u32[]{:S(2)}) copy-start(s32[128]{0:T(128)} %param.5) | copy-start | bytes 1540
  7.2 207.0 %all-gather.4.cloned.1.call-start = ((), (), s32[]{:S(2)}) async-start(), calls=%async_computation.5 | async-start | bytes 8519680 | tf_op jit(solution)/shard_map/all_gather | solution.py:46
  24.1 6.5 all-to-all-start
  223.3 185.4 %all-to-all-start.2 = ((f32[64,1,128]{2,1,0:T(1,128)}), f32[64,1,128]{2,1,0:T(1,128)S(1)}, u32[]{:S(2)}, u32[]{:S(2)}) async-start(f32[64,1,128]{2,1,0:T(1,128)} %stack.2), calls=%async_computation.2 | async-start | bytes 65536 | tf_op jit(solution)/shard_map/all_to_all | solution.py:58
  227.9 228.3 %all-reduce.2.cloned.1.call-start = ((), (), s32[]{:S(2)}) async-start(), calls=%async_computation.6 | async-start | bytes 2097152 | tf_op jit(solution)/shard_map/psum | solution.py:79
  417.0 408.6 %reduce-scatter.2.cloned.1.call-start = ((), (), s32[]{:S(2)}) async-start(), calls=%async_computation.7 | async-start | bytes 2129920 | tf_op jit(solution)/shard_map/reduce_scatter | solution.py:85
Sparse Core Ops, SparseCore 0:
  21.1 148.5 all-gather.3
  417.1 39.0 all-reduce.1
  459.3 366.2 reduce-scatter.1
